TPU v7x, 32 devices: a whole 2x2x4 slice. The times are simulated.
32 devices in a mesh: dp: 4 (over y, x), seq: 8 (over z, core).
Axes of the slice: x: 2, y: 2, z: 4, core: 2. Of those that a mesh axis runs over, the one named last changes fastest.
Arguments:
- query_rows: bfloat16 [4, 1024, 1536], P('dp', 'seq'), may hold values from -6 to 6
- key_rows: bfloat16 [4, 1024, 1536], P('dp', 'seq'), may hold values from -6 to 6
- value_rows: bfloat16 [4, 1024, 1536], P('dp', 'seq'), may hold values from -6 to 6
- out_grad: bfloat16 [4, 1024, 1536], P('dp', 'seq'), may hold values from -36 to 36
- query_gain: float32 [128], replicated, may hold values from 0.5 to 5.5
- key_gain: float32 [128], replicated, may hold values from 0.5 to 5.5
- lengths: int32 [4, 16], P('dp'), may hold values from 1 to 128, 1024 in all within a row
Outputs:
- query_grad: bfloat16 [4, 1024, 1536], P('dp', 'seq')
- key_grad: bfloat16 [4, 1024, 1536], P('dp', 'seq')
- value_grad: bfloat16 [4, 1024, 1536], P('dp', 'seq')
- gain_grads: float32 [2, 128], replicated
Inputs may be any that keep to these rules, and one draw needn't show every extreme that they name: The 16 lengths of a pack sum to 1024, and some sample of every pack has exactly 128 tokens.
All inputs are finite; a program needn't handle non-finite values.
Results may differ from a plain program's by a relative error of at most 0.023.
The roundings to bfloat16 on the way count: a program that leaves them out, or rounds other values in their place, can miss the bound.
Values may be sent and summed in bfloat16 or wider, within the bound.
A program may use at most 64 MiB of HBM per device.

v0:
```python
import jax
import jax.numpy as jnp
from jax import lax
from jax.sharding import PartitionSpec as P

H = 12
DH = 128
SPAN = 1


EPSILON = 1e-06
MASKED = -1e30


def from_behind(block, axis, distance):
    devices = range(lax.axis_size(axis))
    route = [(i - distance, i) for i in devices if i - distance in devices]
    return lax.ppermute(block, axis, route)


def product(pattern, left_side, right_side):
    return jnp.einsum(pattern, left_side, right_side, preferred_element_type=jnp.float32)


def normalize(entries, norm_gain):
    row_count = entries.shape[0]
    widened = entries.astype(jnp.float32).reshape(row_count, H, DH)
    inverse = lax.rsqrt(jnp.mean(widened * widened, axis=2, keepdims=True) + EPSILON)
    unit_rows = widened * inverse
    return (
        (unit_rows * norm_gain).astype(jnp.bfloat16).reshape(row_count, H * DH),
        unit_rows,
        inverse,
    )


def norm_back(grad_rows, unit_rows, inverse, norm_gain):
    scaled = grad_rows * norm_gain
    inner_mean = jnp.mean(scaled * unit_rows, axis=2, keepdims=True)
    result = inverse * (scaled - unit_rows * inner_mean)
    return (
        result.reshape(grad_rows.shape[0], H * DH).astype(jnp.bfloat16),
        jnp.sum(grad_rows * unit_rows, axis=(0, 1)),
    )


def segment_of(positions, lengths, extent):
    sample_ends = jnp.cumsum(lengths)
    number = jnp.sum((sample_ends[None, :] <= positions[:, None]).astype(jnp.int32), axis=1)
    inside = (positions >= 0) & (positions < extent)
    return jnp.where(inside, number, -1)


def forward_band(queries, band_keys, band_values, seg_query, seg_band):
    row_count = queries.shape[0]
    factor = DH ** (-0.5)
    scores = (
        product("qhd,khd->hqk", queries.reshape(row_count, H, DH), band_keys.reshape(-1, H, DH))
        * factor
    )
    matching = seg_query[:, None] == seg_band[None, :]
    scores = jnp.where(matching[None], scores, MASKED)
    highest = jnp.max(scores, axis=2, keepdims=True)
    summed = jnp.sum(jnp.exp(scores - highest), axis=2, keepdims=True)
    log_total = highest + jnp.log(summed)
    weights = jnp.exp(scores - log_total)
    weights_half = weights.astype(jnp.bfloat16)
    attended = product("hqk,khd->qhd", weights_half, band_values.reshape(-1, H, DH)).astype(
        jnp.bfloat16
    )
    return (weights, weights_half, log_total, attended)


def backward_band(queries, band_keys, band_values, grad_out, weights, attended):
    row_count = queries.shape[0]
    factor = DH ** (-0.5)
    grad_heads = grad_out.reshape(row_count, H, DH)
    row_dot = jnp.sum(grad_heads.astype(jnp.float32) * attended.astype(jnp.float32), axis=2)
    row_dot = jnp.transpose(row_dot)[:, :, None]
    grad_weights = product("qhd,khd->hqk", grad_heads, band_values.reshape(-1, H, DH))
    grad_scores = (weights * (grad_weights - row_dot)).astype(jnp.bfloat16)
    grad_query = product("hqk,khd->qhd", grad_scores, band_keys.reshape(-1, H, DH)) * factor
    return (grad_query, row_dot)


def key_side(band_queries, band_grads, band_stats, own_keys, own_values, seg_band, seg_own):
    factor = DH ** (-0.5)
    band_count = band_queries.shape[0]
    query_heads = band_queries.reshape(band_count, H, DH)
    grad_heads = band_grads.reshape(band_count, H, DH)
    scores = product("qhd,khd->hqk", query_heads, own_keys.reshape(-1, H, DH)) * factor
    matching = seg_band[:, None] == seg_own[None, :]
    log_total = band_stats[0][:, :, None]
    row_dot = band_stats[1][:, :, None]
    weights = jnp.where(matching[None], jnp.exp(scores - log_total), 0.0)
    weights_half = weights.astype(jnp.bfloat16)
    grad_weights = product("qhd,khd->hqk", grad_heads, own_values.reshape(-1, H, DH))
    grad_scores = (weights * (grad_weights - row_dot)).astype(jnp.bfloat16)
    key_terms = product("hqk,qhd->khd", grad_scores, query_heads) * factor
    value_terms = product("hqk,qhd->khd", weights_half, grad_heads)
    return (key_terms, value_terms)


def body(query_rows, key_rows, value_rows, out_grad, query_gain, key_gain, lengths):
    row_count = query_rows.shape[1]
    width = H * DH
    reach = SPAN * row_count
    extent = row_count * lax.axis_size("seq")
    offset = lax.axis_index("seq") * row_count
    own_positions = offset + jnp.arange(row_count, dtype=jnp.int32)
    band_positions = offset - reach + jnp.arange(row_count + 2 * reach, dtype=jnp.int32)
    seg_own = segment_of(own_positions, lengths[0], extent)
    seg_band = segment_of(band_positions, lengths[0], extent)
    q_norm, q_unit, q_inverse = normalize(query_rows[0], query_gain)
    k_norm, k_unit, k_inverse = normalize(key_rows[0], key_gain)
    own_pair = jnp.stack([k_norm, value_rows[0]])
    pieces = []
    for step in range(2 * SPAN + 1):
        if step == SPAN:
            pieces.append(own_pair)
        else:
            pieces.append(from_behind(own_pair, "seq", SPAN - step))
    band_pair = jnp.concatenate(pieces, axis=1)
    weights, weights_half, log_total, attended = forward_band(
        q_norm, band_pair[0], band_pair[1], seg_own, seg_band
    )
    grads = out_grad[0]
    grad_query, row_dot = backward_band(
        q_norm, band_pair[0], band_pair[1], grads, weights, attended
    )
    row_stats = jnp.stack([log_total[:, :, 0], row_dot[:, :, 0]])
    query_pair = jnp.stack([q_norm, grads])
    query_pieces = []
    stat_pieces = []
    for step in range(2 * SPAN + 1):
        if step == SPAN:
            query_pieces.append(query_pair)
            stat_pieces.append(row_stats)
        else:
            query_pieces.append(from_behind(query_pair, "seq", SPAN - step))
            stat_pieces.append(from_behind(row_stats, "seq", SPAN - step))
    band_queries = jnp.concatenate(query_pieces, axis=1)
    band_stats = jnp.concatenate(stat_pieces, axis=2)
    key_terms, value_terms = key_side(
        band_queries[0], band_queries[1], band_stats, k_norm, value_rows[0], seg_band, seg_own
    )
    key_total = key_terms.reshape(row_count, width)
    value_total = value_terms.reshape(row_count, width)
    d_query, q_gain_grad = norm_back(grad_query, q_unit, q_inverse, query_gain)
    d_key, k_gain_grad = norm_back(key_total.reshape(row_count, H, DH), k_unit, k_inverse, key_gain)
    d_value = value_total.astype(jnp.bfloat16)
    gain_grads = lax.psum(jnp.stack([q_gain_grad, k_gain_grad]), ("dp", "seq"))
    return (d_query[None], d_key[None], d_value[None], gain_grads)


def solution(mesh):
    placed = (
        P("dp", "seq", None),
        P("dp", "seq", None),
        P("dp", "seq", None),
        P("dp", "seq", None),
        P(),
        P(),
        P("dp", None),
    )
    return jax.shard_map(
        body,
        mesh=mesh,
        in_specs=placed,
        out_specs=(P("dp", "seq", None), P("dp", "seq", None), P("dp", "seq", None), P()),
        check_vma=False,
    )
```

profile of v0, /device:TPU:0, one launch (start us, length us, event | category | flops | bytes accessed | tf_op | source)
XLA Modules:
  0.0 98.2 jit_solution(13048086161903132749)
XLA Ops:
  0.6 1.2 %copy.61 = bf16[1,128,1536]{1,2,0:T(8,128)(2,1)S(1)} copy(bf16[1,128,1536]{2,1,0:T(8,128)(2,1)} %param.9) | data formatting | bytes 786432 | tf_op args[2]
  1.9 0.7 broadcast_bitcast_fusion.1
  2.6 1.2 %copy.60 = bf16[1,128,1536]{1,2,0:T(8,128)(2,1)S(1)} copy(bf16[1,128,1536]{2,1,0:T(8,128)(2,1)} %param.8) | data formatting | bytes 786432 | tf_op args[1]
  3.8 1.0 multiply_reduce_fusion
  4.8 0.3 fusion.34
  5.1 0.9 pad_maximum_fusion.2
  6.1 1.3 %collective-permute-start.1 = (bf16[2,128,1536]{1,2,0:T(8,128)(2,1)}, bf16[2,128,1536]{1,2,0:T(8,128)(2,1)S(1)}, u32[]{:S(2)}, u32[]{:S(2)}) collective-permute-start(bf16[2,128,1536]{1,2,0:T(8,128)(2,1)} %pad_maximum_fusion.2), channel_id=1, source_target_pairs={{1,0},{2,1},{3,2},{4,3},{5,4},{6,5},{7,6},{9,8},{10,9},{11,10},{12... | collective-permute-start | bytes 2359304 | tf_op jit(solution)/shard_map/ppermute | solution.py:18
  7.3 3.9 %collective-permute-start = (bf16[2,128,1536]{1,2,0:T(8,128)(2,1)}, bf16[2,128,1536]{1,2,0:T(8,128)(2,1)}, u32[]{:S(2)}, u32[]{:S(2)}) collective-permute-start(bf16[2,128,1536]{1,2,0:T(8,128)(2,1)} %pad_maximum_fusion.2), channel_id=1, source_target_pairs={{0,1},{1,2},{2,3},{3,4},{4,5},{5,6},{6,7},{8,9},{9,10},{10,11},{11... | collective-permute-start | bytes 2359304 | tf_op jit(solution)/shard_map/ppermute | solution.py:18
  11.3 0.2 copy.59
  11.5 0.1 multiply_reduce_fusion.1
  11.7 0.2 copy.65
  11.9 0.3 fusion.29
  12.2 0.7 copy-done.8
  12.9 1.0 pad_maximum_fusion.3
  13.9 1.3 %collective-permute-start.3 = (bf16[2,128,1536]{1,2,0:T(8,128)(2,1)}, bf16[2,128,1536]{1,2,0:T(8,128)(2,1)}, u32[]{:S(2)}, u32[]{:S(2)}) collective-permute-start(bf16[2,128,1536]{1,2,0:T(8,128)(2,1)} %pad_maximum_fusion.3), channel_id=1, source_target_pairs={{1,0},{2,1},{3,2},{4,3},{5,4},{6,5},{7,6},{9,8},{10,9},{11,10},{12... | collective-permute-start | bytes 2359304 | tf_op jit(solution)/shard_map/ppermute | solution.py:18
  15.2 5.2 %collective-permute-start.2 = (bf16[2,128,1536]{1,2,0:T(8,128)(2,1)}, bf16[2,128,1536]{1,2,0:T(8,128)(2,1)}, u32[]{:S(2)}, u32[]{:S(2)}) collective-permute-start(bf16[2,128,1536]{1,2,0:T(8,128)(2,1)} %pad_maximum_fusion.3), channel_id=1, source_target_pairs={{0,1},{1,2},{2,3},{3,4},{4,5},{5,6},{6,7},{8,9},{9,10},{10,11},{11... | collective-permute-start | bytes 2359304 | tf_op jit(solution)/shard_map/ppermute | solution.py:18
  20.4 0.5 broadcast_multiply_fusion.3
  20.9 0.5 broadcast_multiply_fusion.2
  21.4 0.7 copy.62
  22.2 0.1 reduce
  22.3 0.1 convert_reduce_fusion.1
  22.5 0.1 broadcast_compare_fusion.1
  22.6 0.7 broadcast_compare_fusion
  23.4 1.4 %pad_maximum_fusion = bf16[2,384,1536]{1,2,0:T(8,128)(2,1)S(1)} fusion(bf16[2,128,1536]{1,2,0:T(8,128)(2,1)S(1)} %collective-permute-done.1, bf16[1,128,1536]{1,2,0:T(8,128)(2,1)S(1)} %copy.61, bf16[1,128,1536]{1,2,0:T(8,128)(2,1)S(1)} %fusion.34, bf16[2,128,1536]{1,2,0:T(8,128)(2,1)} %collective-permute-done), kind=kLoop, calls=%fused_computation | loop fusion | flops 9437184 | bytes 4718592 | tf_op jit(solution)/shard_map/concatenate | solution.py:123
  24.8 0.2 fusion.45
  25.1 0.7 fusion.46
  25.8 0.7 exponential_reduce_fusion
  26.6 0.7 fusion.8
  27.3 0.6 copy-done.16
  27.9 0.6 pad_maximum_fusion.5
  28.5 1.3 %collective-permute-start.5 = (f32[2,12,128]{2,1,0:T(8,128)}, f32[2,12,128]{2,1,0:T(8,128)}, u32[]{:S(2)}, u32[]{:S(2)}) collective-permute-start(f32[2,12,128]{2,1,0:T(8,128)} %pad_maximum_fusion.5), channel_id=1, source_target_pairs={{1,0},{2,1},{3,2},{4,3},{5,4},{6,5},{7,6},{9,8},{10,9},{11,10},{12... | collective-permute-start | bytes 36872 | tf_op jit(solution)/shard_map/ppermute | solution.py:18
  29.8 4.0 %collective-permute-start.4 = (f32[2,12,128]{2,1,0:T(8,128)}, f32[2,12,128]{2,1,0:T(8,128)}, u32[]{:S(2)}, u32[]{:S(2)}) collective-permute-start(f32[2,12,128]{2,1,0:T(8,128)} %pad_maximum_fusion.5), channel_id=1, source_target_pairs={{0,1},{1,2},{2,3},{3,4},{4,5},{5,6},{6,7},{8,9},{9,10},{10,11},{11... | collective-permute-start | bytes 36872 | tf_op jit(solution)/shard_map/ppermute | solution.py:18
  33.8 4.2 %fusion.24 = (f32[128]{0:T(128)}, f32[128,12]{0,1:T(8,128)}, f32[12,128,128]{2,1,0:T(8,128)}) fusion(f32[128,12,128]{0,2,1:T(8,128)S(1)} %get-tuple-element.25, f32[128,12]{0,1:T(8,128)S(1)} %add_rsqrt_fusion.1, f32[128]{0:T(128)} %broadcast_multiply_fusion.3, bf16[384,12,128]{0,2,1:T(8,128)(2,1)} %bitcast.93, f32[12,128,384]{2,1,0:T(8,128)S(1)} %get-tuple-element.35, ...), kind=kOutput, calls=%fused_computation.36 | convolution fusion | flops 305723776 | bytes 6710272 | tf_op jit(solution)/shard_map/hqk,khd->qhd/dot_general | solution.py:22
  38.0 0.7 broadcast_multiply_fusion.1
  38.7 1.8 %pad_maximum_fusion.1 = bf16[2,384,1536]{1,2,0:T(8,128)(2,1)S(1)} fusion(bf16[2,128,1536]{1,2,0:T(8,128)(2,1)} %collective-permute-done.3, bf16[1,128,1536]{1,2,0:T(8,128)(2,1)S(1)} %copy.65, bf16[1,128,1536]{1,2,0:T(8,128)(2,1)} %copy-done.8, bf16[2,128,1536]{1,2,0:T(8,128)(2,1)} %collective-permute-done.2), kind=kLoop, calls=%fused_computation.1 | loop fusion | flops 9437184 | bytes 4718592 | tf_op jit(solution)/shard_map/concatenate | solution.py:142
  40.6 0.2 fusion.44
  40.9 0.8 copy-done.2
  41.7 2.0 %fusion.35 = f32[12,384,128]{2,1,0:T(8,128)} fusion(bf16[384,12,128]{0,2,1:T(8,128)(2,1)S(1)} %bitcast.98, f32[128,12,128]{0,2,1:T(8,128)S(1)} %copy-done.2, f32[128]{0:T(128)S(1)} %copy-done.22, f32[128,12]{0,1:T(8,128)S(1)} %copy-done.14), kind=kOutput, calls=%fused_computation.57 | convolution fusion | flops 151584768 | bytes 4332032 | tf_op jit(solution)/shard_map/qhd,khd->hqk/dot_general | solution.py:22
  43.7 0.2 fusion.32
  43.9 0.9 copy.75
  44.9 0.7 pad_maximum_fusion.4
  45.6 0.6 slice_bitcast_fusion.1
  46.2 3.5 %convolution_convert_fusion = bf16[12,128,128]{2,1,0:T(8,128)(2,1)} fusion(bf16[384,12,128]{0,2,1:T(8,128)(2,1)S(1)} %bitcast.105, f32[12,384,128]{2,1,0:T(8,128)} %fusion.35, f32[12,384]{1,0:T(8,128)S(1)} %get-tuple-element.32, pred[384,128]{1,0:T(8,128)(4,1)} %broadcast_compare_fusion), kind=kOutput, calls=%fused_computation.13 | convolution fusion | flops 153550848 | bytes 3999744 | tf_op jit(solution)/shard_map/hqk,qhd->khd/dot_general | solution.py:22
  49.7 5.0 %fusion.23 = (f32[128]{0:T(128)}, f32[128,12]{0,1:T(8,128)S(1)}, f32[12,128,128]{2,1,0:T(8,128)}) fusion(f32[128,12,128]{0,2,1:T(8,128)S(1)} %copy-done.3, f32[128,12]{0,1:T(8,128)S(1)} %copy-done.15, f32[128]{0:T(128)} %broadcast_multiply_fusion.2, bf16[384,12,128]{0,2,1:T(8,128)(2,1)S(1)} %bitcast.99, f32[12,384,128]{2,1,0:T(8,128)} %fusion.35, ...), kind=kOutput, calls=%fused_computation.34 | convolution fusion | flops 306903424 | bytes 6784000 | tf_op jit(solution)/shard_map/hqk,qhd->khd/dot_general | solution.py:22
  54.8 1.4 %fusion.27 = bf16[128,12,128]{0,2,1:T(8,128)(2,1)S(1)} fusion(f32[12,128,128]{2,1,0:T(8,128)} %get-tuple-element.37, f32[128,12,128]{0,2,1:T(8,128)S(1)} %copy-done.3, f32[128,12]{0,1:T(8,128)S(1)} %broadcast_multiply_fusion, f32[128]{0:T(128)} %broadcast_multiply_fusion.2, f32[128,12]{0,1:T(8,128)S(1)} %copy-done.15), kind=kLoop, calls=%fused_computation.41 | loop fusion | flops 1179648 | bytes 1978880 | tf_op jit(solution)/shard_map/convert_element_type | solution.py:42
  56.2 0.9 copy.76
  57.1 0.9 copy.77
  58.1 40.1 %psum.7 = f32[2,128]{1,0:T(2,128)} all-reduce(f32[2,128]{1,0:T(2,128)S(1)} %pad_maximum_fusion.6), channel_id=1, replica_groups=mesh['dp'=4,'seq'=8] {'dp','seq'}, use_global_device_ids=true, to_apply=%region_12.13 | all-reduce | flops 256 | bytes 2048 | tf_op jit(solution)/shard_map/psum | solution.py:152
  (65 shorter events, 0.3 us)
Async XLA Ops:
  1.9 21.5 %copy-start.6 = (bf16[1,128,1536]{1,2,0:T(8,128)(2,1)}, bf16[1,128,1536]{1,2,0:T(8,128)(2,1)S(1)}, u32[]{:S(2)}) copy-start(bf16[1,128,1536]{1,2,0:T(8,128)(2,1)S(1)} %copy.61) | copy-start | bytes 1179652
  1.9 9.4 %copy-start.10 = (bf16[1,128,1536]{2,1,0:T(8,128)(2,1)S(1)}, bf16[1,128,1536]{2,1,0:T(8,128)(2,1)}, u32[]{:S(2)}) copy-start(bf16[1,128,1536]{2,1,0:T(8,128)(2,1)} %param.7) | copy-start | bytes 1179652
  4.8 6.8 %copy-start.11 = (bf16[1,128,1536]{2,1,0:T(8,128)(2,1)S(1)}, bf16[1,128,1536]{2,1,0:T(8,128)(2,1)}, u32[]{:S(2)}) copy-start(bf16[1,128,1536]{2,1,0:T(8,128)(2,1)} %param.10) | copy-start | bytes 1179652
  4.8 6.8 %copy-start.13 = (f32[128,12]{0,1:T(8,128)}, f32[128,12]{0,1:T(8,128)S(1)}, u32[]{:S(2)}) copy-start(f32[128,12]{0,1:T(8,128)S(1)} %add_rsqrt_fusion) | copy-start | bytes 18436
  5.1 6.8 %copy-start.20 = (f32[128]{0:T(128)S(1)}, f32[128]{0:T(128)}, u32[]{:S(2)}) copy-start(f32[128]{0:T(128)} %param.11) | copy-start | bytes 1540
  6.1 17.3 %collective-permute-start.1 = (bf16[2,128,1536]{1,2,0:T(8,128)(2,1)}, bf16[2,128,1536]{1,2,0:T(8,128)(2,1)S(1)}, u32[]{:S(2)}, u32[]{:S(2)}) collective-permute-start(bf16[2,128,1536]{1,2,0:T(8,128)(2,1)} %pad_maximum_fusion.2), channel_id=1, source_target_pairs={{1,0},{2,1},{3,2},{4,3},{5,4},{6,5},{7,6},{9,8},{10,9},{11,10},{12... | collective-permute-start | bytes 2359304 | tf_op jit(solution)/shard_map/ppermute | solution.py:18
  7.3 16.0 %collective-permute-start = (bf16[2,128,1536]{1,2,0:T(8,128)(2,1)}, bf16[2,128,1536]{1,2,0:T(8,128)(2,1)}, u32[]{:S(2)}, u32[]{:S(2)}) collective-permute-start(bf16[2,128,1536]{1,2,0:T(8,128)(2,1)} %pad_maximum_fusion.2), channel_id=1, source_target_pairs={{0,1},{1,2},{2,3},{3,4},{4,5},{5,6},{6,7},{8,9},{9,10},{10,11},{11... | collective-permute-start | bytes 2359304 | tf_op jit(solution)/shard_map/ppermute | solution.py:18
  11.5 9.4 %copy-start.21 = (f32[128]{0:T(128)S(1)}, f32[128]{0:T(128)}, u32[]{:S(2)}) copy-start(f32[128]{0:T(128)} %param.12) | copy-start | bytes 1540
  12.2 0.7 copy-start.8
  13.9 24.8 %collective-permute-start.3 = (bf16[2,128,1536]{1,2,0:T(8,128)(2,1)}, bf16[2,128,1536]{1,2,0:T(8,128)(2,1)}, u32[]{:S(2)}, u32[]{:S(2)}) collective-permute-start(bf16[2,128,1536]{1,2,0:T(8,128)(2,1)} %pad_maximum_fusion.3), channel_id=1, source_target_pairs={{1,0},{2,1},{3,2},{4,3},{5,4},{6,5},{7,6},{9,8},{10,9},{11,10},{12... | collective-permute-start | bytes 2359304 | tf_op jit(solution)/shard_map/ppermute | solution.py:18
  15.2 23.6 %collective-permute-start.2 = (bf16[2,128,1536]{1,2,0:T(8,128)(2,1)}, bf16[2,128,1536]{1,2,0:T(8,128)(2,1)}, u32[]{:S(2)}, u32[]{:S(2)}) collective-permute-start(bf16[2,128,1536]{1,2,0:T(8,128)(2,1)} %pad_maximum_fusion.3), channel_id=1, source_target_pairs={{0,1},{1,2},{2,3},{3,4},{4,5},{5,6},{6,7},{8,9},{9,10},{10,11},{11... | collective-permute-start | bytes 2359304 | tf_op jit(solution)/shard_map/ppermute | solution.py:18
  25.1 1.5 %copy-start = (bf16[1,384,1536]{1,2,0:T(8,128)(2,1)}, bf16[1,384,1536]{1,2,0:T(8,128)(2,1)S(1)}, u32[]{:S(2)}) copy-start(bf16[1,384,1536]{1,2,0:T(8,128)(2,1)S(1)} %get-tuple-element.31) | copy-start | bytes 3538948
  25.1 1.5 %copy-start.1 = (bf16[1,384,1536]{1,2,0:T(8,128)(2,1)}, bf16[1,384,1536]{1,2,0:T(8,128)(2,1)S(1)}, u32[]{:S(2)}) copy-start(bf16[1,384,1536]{1,2,0:T(8,128)(2,1)S(1)} %get-tuple-element.30) | copy-start | bytes 3538948
  27.3 0.6 copy-start.16
  28.5 16.3 %collective-permute-start.5 = (f32[2,12,128]{2,1,0:T(8,128)}, f32[2,12,128]{2,1,0:T(8,128)}, u32[]{:S(2)}, u32[]{:S(2)}) collective-permute-start(f32[2,12,128]{2,1,0:T(8,128)} %pad_maximum_fusion.5), channel_id=1, source_target_pairs={{1,0},{2,1},{3,2},{4,3},{5,4},{6,5},{7,6},{9,8},{10,9},{11,10},{12... | collective-permute-start | bytes 36872 | tf_op jit(solution)/shard_map/ppermute | solution.py:18
  29.8 15.1 %collective-permute-start.4 = (f32[2,12,128]{2,1,0:T(8,128)}, f32[2,12,128]{2,1,0:T(8,128)}, u32[]{:S(2)}, u32[]{:S(2)}) collective-permute-start(f32[2,12,128]{2,1,0:T(8,128)} %pad_maximum_fusion.5), channel_id=1, source_target_pairs={{0,1},{1,2},{2,3},{3,4},{4,5},{5,6},{6,7},{8,9},{9,10},{10,11},{11... | collective-permute-start | bytes 36872 | tf_op jit(solution)/shard_map/ppermute | solution.py:18
  40.5 1.1 %copy-start.2 = (f32[128,12,128]{0,2,1:T(8,128)S(1)}, f32[128,12,128]{0,2,1:T(8,128)}, u32[]{:S(2)}) copy-start(f32[128,12,128]{0,2,1:T(8,128)} %get-tuple-element.27) | copy-start | bytes 2359300
  40.6 1.1 %copy-start.14 = (f32[128,12]{0,1:T(8,128)S(1)}, f32[128,12]{0,1:T(8,128)}, u32[]{:S(2)}) copy-start(f32[128,12]{0,1:T(8,128)} %copy-done.13) | copy-start | bytes 18436
  40.6 1.1 %copy-start.22 = (f32[128]{0:T(128)S(1)}, f32[128]{0:T(128)}, u32[]{:S(2)}) copy-start(f32[128]{0:T(128)} %param.12) | copy-start | bytes 1540
  40.8 3.1 %copy-start.4 = (bf16[1,384,1536]{1,2,0:T(8,128)(2,1)}, bf16[1,384,1536]{1,2,0:T(8,128)(2,1)S(1)}, u32[]{:S(2)}) copy-start(bf16[1,384,1536]{1,2,0:T(8,128)(2,1)S(1)} %get-tuple-element.29) | copy-start | bytes 3538948
  40.8 2.9 %copy-start.9 = (f32[12,128,128]{2,1,0:T(8,128)S(1)}, f32[12,128,128]{2,1,0:T(8,128)}, u32[]{:S(2)}) copy-start(f32[12,128,128]{2,1,0:T(8,128)} %get-tuple-element.36) | copy-start | bytes 2359300
  40.8 2.8 %copy-start.19 = (f32[128]{0:T(128)S(1)}, f32[128]{0:T(128)}, u32[]{:S(2)}) copy-start(f32[128]{0:T(128)} %broadcast_multiply_fusion.3) | copy-start | bytes 1540
  43.7 1.2 %copy-start.17 = (f32[128,12]{0,1:T(8,128)S(1)}, f32[128,12]{0,1:T(8,128)}, u32[]{:S(2)}) copy-start(f32[128,12]{0,1:T(8,128)} %copy-done.16) | copy-start | bytes 18436
  46.2 3.5 %copy-start.18 = (f32[12,384]{1,0:T(8,128)}, f32[12,384]{1,0:T(8,128)S(1)}, u32[]{:S(2)}) copy-start(f32[12,384]{1,0:T(8,128)S(1)} %get-tuple-element.32) | copy-start | bytes 55300
  46.2 3.5 %copy-start.3 = (f32[128,12,128]{0,2,1:T(8,128)S(1)}, f32[128,12,128]{0,2,1:T(8,128)}, u32[]{:S(2)}) copy-start(f32[128,12,128]{0,2,1:T(8,128)} %get-tuple-element.27) | copy-start | bytes 2359300
  46.2 3.5 %copy-start.5 = (bf16[1,384,1536]{1,2,0:T(8,128)(2,1)S(1)}, bf16[1,384,1536]{1,2,0:T(8,128)(2,1)}, u32[]{:S(2)}) copy-start(bf16[1,384,1536]{1,2,0:T(8,128)(2,1)} %copy-done.4) | copy-start | bytes 3538948
  46.2 3.5 %copy-start.7 = (bf16[1,128,1536]{1,2,0:T(8,128)(2,1)S(1)}, bf16[1,128,1536]{1,2,0:T(8,128)(2,1)}, u32[]{:S(2)}) copy-start(bf16[1,128,1536]{1,2,0:T(8,128)(2,1)} %copy-done.6) | copy-start | bytes 1179652
  46.2 3.5 %copy-start.15 = (f32[128,12]{0,1:T(8,128)S(1)}, f32[128,12]{0,1:T(8,128)}, u32[]{:S(2)}) copy-start(f32[128,12]{0,1:T(8,128)} %copy-done.13) | copy-start | bytes 18436
  54.8 2.3 %copy-start.12 = (bf16[12,128,128]{2,1,0:T(8,128)(2,1)S(1)}, bf16[12,128,128]{2,1,0:T(8,128)(2,1)}, u32[]{:S(2)}) copy-start(bf16[12,128,128]{2,1,0:T(8,128)(2,1)} %convolution_convert_fusion) | copy-start | bytes 1179652
  54.8 3.3 %copy-start.23 = (f32[128]{0:T(128)S(1)}, f32[128]{0:T(128)}, u32[]{:S(2)}) copy-start(f32[128]{0:T(128)} %get-tuple-element.20) | copy-start | bytes 1540
  54.8 3.3 %copy-start.24 = (f32[128]{0:T(128)S(1)}, f32[128]{0:T(128)}, u32[]{:S(2)}) copy-start(f32[128]{0:T(128)} %get-tuple-element.22) | copy-start | bytes 1540
where the time goes:
time: 98.8 us; the launch traced here: 98.2 us
  blocking collectives  40.1 us (41%)
  starting transfers between devices  17 us (17%)
  matrix products  16.2 us (16%)
  other arithmetic  13.4 us (14%)
  local copies, waits for them, and re-layouts  10.4 us (11%)
  between operations  1.01 us (1%)
    psum x1, blocking collectives, body(): gain_grads = lax.psum(jnp.stack([q_gain_grad, k_gain_grad]), ('dp', 'seq'))  40.1 us
    ppermute x6, starting transfers between devices, from_behind(): return lax.ppermute(block, axis, route)  17 us
    dot_general x6, matrix products, product(): jnp.einsum(pattern, left_side, right_side, preferred_element_type=jnp.flo...  16.2 us
    unnamed x57, local copies, waits for them, and re-layouts  7.9 us
  transfers between devices with their start and end apart: 6, of which 0 were waited for; matrix products, arithmetic and copies ran while one was open for 20% of the time, Pallas kernels for 0%

commit v1 on v0

v1 whole, which is shorter than its diff:
```python
import functools

import jax
import jax.numpy as jnp
from jax import lax
from jax.experimental import pallas as pl
from jax.experimental.pallas import tpu as pltpu
from jax.sharding import PartitionSpec as P

DH = 128
EPSILON = 1e-06
MASKED = -1e30
HEADS_STEP = 2


def norm_back(grad, unit, inverse, gain):
    scaled = grad * gain
    inner = jnp.mean(scaled * unit, axis=1, keepdims=True)
    return (inverse * (scaled - unit * inner)).astype(jnp.bfloat16)


def kernel(
    rows, width, samples, n_seq, n_dp,
    q_ref, k_ref, v_ref, g_ref, qgain_ref, kgain_ref, len_ref,
    dq_ref, dk_ref, dv_ref, gain_ref,
    win, bias, owned, own_out, ret_send, ret_recv, gain_acc, seq_gain, dp_gain,
    load_sem, send_sem, recv_sem, back_send_sem, back_recv_sem, store_sem,
    seq_send_sem, seq_recv_sem, dp_send_sem, dp_recv_sem,
):
    half = rows // 2
    window = 2 * rows
    cols_step = HEADS_STEP * DH
    steps = width // cols_step
    factor = DH ** (-0.5)
    me = lax.axis_index("seq")
    my_dp = lax.axis_index("dp")
    has_left = me > 0
    has_right = me < n_seq - 1
    inputs = (q_ref, k_ref, v_ref, g_ref)
    outputs = (dq_ref, dk_ref, dv_ref)

    barrier = pltpu.get_barrier_semaphore()
    for d in range(1, n_seq):
        pl.semaphore_signal(barrier, inc=1, device_id={"seq": lax.rem(me + d, n_seq)})
    for d in range(1, n_dp):
        pl.semaphore_signal(barrier, inc=1, device_id={"dp": lax.rem(my_dp + d, n_dp)})

    loads = [
        pltpu.make_async_copy(ref.at[0], win.at[a, pl.ds(half, rows)], load_sem.at[a])
        for a, ref in enumerate(inputs)
    ]
    for load in loads:
        load.start()
    pl.semaphore_wait(barrier, n_seq + n_dp - 2)

    def columns(step):
        return pl.ds(pl.multiple_of(step * cols_step, cols_step), cols_step)

    def to_left(a, step):
        return pltpu.make_async_remote_copy(
            inputs[a].at[0, pl.ds(0, half), columns(step)],
            win.at[a, pl.ds(half + rows, half), columns(step)],
            send_sem.at[step, a, 0], recv_sem.at[step, a, 1],
            device_id={"seq": me - 1},
        )

    def to_right(a, step):
        return pltpu.make_async_remote_copy(
            inputs[a].at[0, pl.ds(half, half), columns(step)],
            win.at[a, pl.ds(0, half), columns(step)],
            send_sem.at[step, a, 1], recv_sem.at[step, a, 0],
            device_id={"seq": me + 1},
        )

    def back_left(step):
        return pltpu.make_async_remote_copy(
            ret_send.at[0, :, :, columns(step)],
            ret_recv.at[1, :, :, columns(step)],
            back_send_sem.at[step, 0], back_recv_sem.at[step, 1],
            device_id={"seq": me - 1},
        )

    def back_right(step):
        return pltpu.make_async_remote_copy(
            ret_send.at[1, :, :, columns(step)],
            ret_recv.at[0, :, :, columns(step)],
            back_send_sem.at[step, 1], back_recv_sem.at[step, 0],
            device_id={"seq": me + 1},
        )

    @pl.loop(0, steps)
    def _(step):
        @pl.when(has_right)
        def _():
            for a in range(4):
                to_right(a, step).start()

        @pl.when(has_left)
        def _():
            for a in range(4):
                to_left(a, step).start()

    @pl.when(jnp.logical_not(has_left))
    def _():
        win[:, 0:half, :] = jnp.zeros((4, half, width), jnp.bfloat16)
        ret_recv[0] = jnp.zeros((3, half, width), jnp.bfloat16)

    @pl.when(jnp.logical_not(has_right))
    def _():
        win[:, half + rows:, :] = jnp.zeros((4, half, width), jnp.bfloat16)
        ret_recv[1] = jnp.zeros((3, half, width), jnp.bfloat16)

    first = me * rows
    base = first - half
    far = rows * n_seq + window
    pos_col = base + lax.broadcasted_iota(jnp.int32, (window, 1), 0)
    pos_row = base + lax.broadcasted_iota(jnp.int32, (1, window), 1)
    start_col = jnp.where(pos_col >= 0, 0, -far)
    start_row = jnp.where(pos_row >= 0, 0, -far)
    end_col = jnp.full((window, 1), far, jnp.int32)
    total = jnp.int32(0)
    for s in range(samples):
        total = total + len_ref[0, s]
        start_col = jnp.where(total <= pos_col, total, start_col)
        start_row = jnp.where(total <= pos_row, total, start_row)
        end_col = jnp.where(total > pos_col, jnp.minimum(end_col, total), end_col)
    anchor = jnp.minimum(start_col + half, end_col - 1)
    mine = (anchor >= first) & (anchor < first + rows)
    owned[...] = jnp.where(mine, 1.0, 0.0)
    bias[...] = jnp.where(start_col == start_row, 0.0, MASKED)
    gain_acc[...] = jnp.zeros_like(gain_acc)

    for load in loads:
        load.wait()

    def one_head(head):
        cols = pl.ds(pl.multiple_of(head * DH, DH), DH)
        q_gain = qgain_ref[...]
        k_gain = kgain_ref[...]
        q = win[0, :, cols].astype(jnp.float32)
        k = win[1, :, cols].astype(jnp.float32)
        v = win[2, :, cols]
        grad = win[3, :, cols]
        q_inv = lax.rsqrt(jnp.mean(q * q, axis=1, keepdims=True) + EPSILON)
        k_inv = lax.rsqrt(jnp.mean(k * k, axis=1, keepdims=True) + EPSILON)
        q_unit = q * q_inv
        k_unit = k * k_inv
        q_norm = (q_unit * q_gain).astype(jnp.bfloat16)
        k_norm = (k_unit * k_gain).astype(jnp.bfloat16)
        rowrow = (((1,), (1,)), ((), ()))
        colcol = (((0,), (0,)), ((), ()))
        dot = functools.partial(lax.dot_general, preferred_element_type=jnp.float32)
        scores = dot(q_norm, k_norm, rowrow) * factor + bias[...]
        highest = jnp.max(scores, axis=1, keepdims=True)
        powers = jnp.exp(scores - highest)
        summed = jnp.sum(powers, axis=1, keepdims=True)
        weights = powers * (owned[...] / summed)
        half_weights = weights.astype(jnp.bfloat16)
        attended = jnp.dot(half_weights, v, preferred_element_type=jnp.float32)
        attended = attended.astype(jnp.bfloat16).astype(jnp.float32)
        row_dot = jnp.sum(grad.astype(jnp.float32) * attended, axis=1, keepdims=True)
        grad_weights = dot(grad, v, rowrow)
        grad_scores = (weights * (grad_weights - row_dot)).astype(jnp.bfloat16)
        dq = jnp.dot(grad_scores, k_norm, preferred_element_type=jnp.float32) * factor
        dk = dot(grad_scores, q_norm, colcol) * factor
        dv = dot(half_weights, grad, colcol).astype(jnp.bfloat16)
        gain_acc[0:1] += jnp.sum(dq * q_unit, axis=0, keepdims=True)
        gain_acc[1:2] += jnp.sum(dk * k_unit, axis=0, keepdims=True)
        dq = norm_back(dq, q_unit, q_inv, q_gain)
        dk = norm_back(dk, k_unit, k_inv, k_gain)
        for a, out in enumerate((dq, dk, dv)):
            ret_send[0, a, :, cols] = out[:half]
            own_out[a, :, cols] = out[half:half + rows]
            ret_send[1, a, :, cols] = out[half + rows:]

    @pl.loop(0, steps)
    def _(step):
        @pl.when(has_left)
        def _():
            for a in range(4):
                to_right(a, step).wait_recv()

        @pl.when(has_right)
        def _():
            for a in range(4):
                to_left(a, step).wait_recv()

        for i in range(HEADS_STEP):
            one_head(step * HEADS_STEP + i)

        @pl.when(has_right)
        def _():
            back_right(step).start()

        @pl.when(has_left)
        def _():
            back_left(step).start()

    seq_gain[me] = gain_acc[...]
    for d in range(1, n_seq):
        peer = lax.rem(me + d, n_seq)
        pltpu.make_async_remote_copy(
            seq_gain.at[me], seq_gain.at[me], seq_send_sem.at[d], seq_recv_sem.at[me],
            device_id={"seq": peer},
        ).start()

    def stores(step):
        return [
            pltpu.make_async_copy(
                own_out.at[a, :, columns(step)],
                outputs[a].at[0, :, columns(step)],
                store_sem.at[step, a],
            )
            for a in range(3)
        ]

    def merge(step):
        @pl.when(has_left)
        def _():
            back_right(step).wait_recv()

        @pl.when(has_right)
        def _():
            back_left(step).wait_recv()

        cols = columns(step)
        own_out[:, 0:half, cols] += ret_recv[0, :, :, cols]
        own_out[:, half:rows, cols] += ret_recv[1, :, :, cols]
        for store in stores(step):
            store.start()

    @pl.loop(0, steps - 1)
    def _(step):
        merge(step)

    summed = jnp.zeros_like(gain_acc)
    for d in range(1, n_seq):
        peer = lax.rem(me + d, n_seq)
        pltpu.make_async_remote_copy(
            seq_gain.at[me], seq_gain.at[peer], seq_send_sem.at[d], seq_recv_sem.at[peer],
            device_id={"seq": peer},
        ).wait()
    for i in range(n_seq):
        summed = summed + seq_gain[i]
    dp_gain[my_dp] = summed
    for d in range(1, n_dp):
        peer = lax.rem(my_dp + d, n_dp)
        pltpu.make_async_remote_copy(
            dp_gain.at[my_dp], dp_gain.at[my_dp], dp_send_sem.at[d], dp_recv_sem.at[my_dp],
            device_id={"dp": peer},
        ).start()

    merge(steps - 1)

    for d in range(1, n_dp):
        peer = lax.rem(my_dp + d, n_dp)
        pltpu.make_async_remote_copy(
            dp_gain.at[my_dp], dp_gain.at[peer], dp_send_sem.at[d], dp_recv_sem.at[peer],
            device_id={"dp": peer},
        ).wait()
    summed = jnp.zeros_like(gain_acc)
    for i in range(n_dp):
        summed = summed + dp_gain[i]
    gain_ref[...] = summed[0:2]

    @pl.loop(0, steps)
    def _(step):
        @pl.when(has_right)
        def _():
            for a in range(4):
                to_right(a, step).wait_send()
            back_right(step).wait_send()

        @pl.when(has_left)
        def _():
            for a in range(4):
                to_left(a, step).wait_send()
            back_left(step).wait_send()

        for store in stores(step):
            store.wait()


def body(query_rows, key_rows, value_rows, out_grad, query_gain, key_gain, lengths):
    rows, width = query_rows.shape[1:]
    half, window = rows // 2, 2 * rows
    samples = lengths.shape[1]
    n_seq, n_dp = lax.axis_size("seq"), lax.axis_size("dp")
    steps = width // (HEADS_STEP * DH)
    big = jax.ShapeDtypeStruct((1, rows, width), jnp.bfloat16)
    anywhere = pl.BlockSpec(memory_space=pl.ANY)
    vmem = pl.BlockSpec(memory_space=pltpu.VMEM)
    dma = pltpu.SemaphoreType.DMA
    return pl.pallas_call(
        functools.partial(kernel, rows, width, samples, n_seq, n_dp),
        out_shape=(big, big, big, jax.ShapeDtypeStruct((2, DH), jnp.float32)),
        in_specs=[anywhere] * 4 + [vmem] * 2 + [pl.BlockSpec(memory_space=pltpu.SMEM)],
        out_specs=(anywhere, anywhere, anywhere, vmem),
        scratch_shapes=[
            pltpu.VMEM((4, window, width), jnp.bfloat16),
            pltpu.VMEM((window, window), jnp.float32),
            pltpu.VMEM((window, 1), jnp.float32),
            pltpu.VMEM((3, rows, width), jnp.bfloat16),
            pltpu.VMEM((2, 3, half, width), jnp.bfloat16),
            pltpu.VMEM((2, 3, half, width), jnp.bfloat16),
            pltpu.VMEM((8, DH), jnp.float32),
            pltpu.VMEM((n_seq, 8, DH), jnp.float32),
            pltpu.VMEM((n_dp, 8, DH), jnp.float32),
            dma((4,)),
            dma((steps, 4, 2)),
            dma((steps, 4, 2)),
            dma((steps, 2)),
            dma((steps, 2)),
            dma((steps, 3)),
            dma((n_seq,)),
            dma((n_seq,)),
            dma((n_dp,)),
            dma((n_dp,)),
        ],
        compiler_params=pltpu.CompilerParams(collective_id=0, has_side_effects=True),
    )(
        query_rows, key_rows, value_rows, out_grad,
        query_gain.reshape(1, DH), key_gain.reshape(1, DH), lengths,
    )


def solution(mesh):
    placed = (
        P("dp", "seq", None),
        P("dp", "seq", None),
        P("dp", "seq", None),
        P("dp", "seq", None),
        P(),
        P(),
        P("dp", None),
    )
    return jax.shard_map(
        body,
        mesh=mesh,
        in_specs=placed,
        out_specs=(P("dp", "seq", None), P("dp", "seq", None), P("dp", "seq", None), P()),
        check_vma=False,
    )
```

time: 98.8 us -> 36.7 us (0.37)
  blocking collectives: 40.1 us -> 0 us
  Pallas kernels: 0 us -> 31.6 us
  starting transfers between devices: 17 us -> 0 us
  matrix products: 16.2 us -> 0 us
  other arithmetic: 13.4 us -> 0 us
  local copies, waits for them, and re-layouts: 10.4 us -> 4.27 us
    psum x1 -> x0, blocking collectives: 40.1 us -> none  [body(): gain_grads = lax.psum(jnp.stack([q_gain_grad, k_gain_grad]), ('dp', 'seq'))]
    pallas_call x0 -> x1, Pallas kernels: none -> 31.6 us  [body(): pl.pallas_call(functools.partial(kernel, rows, width, samples, n_seq, n_d...]
    ppermute x6 -> x0, starting transfers between devices: 17 us -> none  [from_behind(): return lax.ppermute(block, axis, route)]
    dot_general x6 -> x0, matrix products: 16.2 us -> none  [product(): jnp.einsum(pattern, left_side, right_side, preferred_element_type=jnp.flo...]
    concatenate x3 -> x0, other arithmetic: 3.99 us -> none  [the longest x1 1.8 us: body(): band_queries = jnp.concatenate(query_pieces, axis=1)]
    unnamed x57 -> x10, local copies, waits for them, and re-layouts: 7.9 us -> 4.27 us
    another operation x6 -> x0, other arithmetic: 2.67 us -> none  [the longest x1 0.96 us: body(): query_pair = jnp.stack([q_norm, grads])]
    convert_element_type x4 -> x0, other arithmetic: 2.15 us -> none  [the longest x2 1.6 us: norm_back(): result.reshape(grad_rows.shape[0], H * DH).astype(jnp.bfloat16)]
  transfers between devices with their start and end apart: 6 -> 0, of which waited for: 0 -> 0; matrix products, arithmetic and copies ran while one was open for 20% -> 0% of each run, Pallas kernels for 0% -> 0%
where the time goes in v1:
time: 36.7 us; the launch traced here: 36.5 us
  Pallas kernels  31.6 us (86%)
  local copies, waits for them, and re-layouts  4.27 us (12%)
  between operations  0.65 us (2%)
    pallas_call x1, Pallas kernels, body(): pl.pallas_call(functools.partial(kernel, rows, width, samples, n_seq, n_d...  31.6 us
    unnamed x10, local copies, waits for them, and re-layouts  4.27 us

profile of v1, /device:TPU:0, one launch (start us, length us, event | category | flops | bytes accessed | tf_op | source)
XLA Modules:
  0.0 36.5 jit_solution(17949803016995013344)
XLA Ops:
  0.6 31.6 %shard_map.102 = (bf16[1,128,1536]{2,1,0:T(8,128)(2,1)}, bf16[1,128,1536]{2,1,0:T(8,128)(2,1)}, bf16[1,128,1536]{2,1,0:T(8,128)(2,1)}, f32[2,128]{1,0:T(2,128)}) custom-call(bf16[1,128,1536]{2,1,0:T(8,128)(2,1)} %q_ref.1, bf16[1,128,1536]{2,1,0:T(8,128)(2,1)} %k_ref.1, bf16[1,128,1536]{2,1,0:T(8,128)(2,1)} %v_ref.1, bf16[1,128,1536]{2,1,0:T(8,128)(2,1)} %g_ref.1, ...), custom_call_target="tpu_custom_call" | custom-call | tf_op jit(solution)/shard_map/pallas_call | solution.py:294
  32.2 0.0 copy-start.1
  32.2 1.8 %copy.15 = bf16[1,128,1536]{2,1,0:T(8,128)(2,1)} copy(bf16[1,128,1536]{2,1,0:T(8,128)(2,1)} %get-tuple-element.8) | data formatting | bytes 786432
  34.0 0.0 copy-done.1
  34.0 0.0 copy-start
  34.0 0.7 %copy.16 = bf16[1,128,1536]{2,1,0:T(8,128)(2,1)} copy(bf16[1,128,1536]{2,1,0:T(8,128)(2,1)S(1)} %copy-done.1) | data formatting | bytes 786432
  34.8 0.4 %copy-done = bf16[1,128,1536]{2,1,0:T(8,128)(2,1)S(1)} copy-done((bf16[1,128,1536]{2,1,0:T(8,128)(2,1)S(1)}, bf16[1,128,1536]{2,1,0:T(8,128)(2,1)}, u32[]{:S(2)}) %copy-start) | copy-done | bytes 393240
  35.2 0.0 copy-start.2
  35.2 0.7 %copy.17 = bf16[1,128,1536]{2,1,0:T(8,128)(2,1)} copy(bf16[1,128,1536]{2,1,0:T(8,128)(2,1)S(1)} %copy-done) | data formatting | bytes 786432
  35.9 0.0 copy-done.2
  35.9 0.6 %copy.18 = f32[2,128]{1,0:T(2,128)} copy(f32[2,128]{1,0:T(2,128)S(1)} %copy-done.2) | data formatting | bytes 2048
Async XLA Ops:
  32.2 1.8 %copy-start.1 = (bf16[1,128,1536]{2,1,0:T(8,128)(2,1)S(1)}, bf16[1,128,1536]{2,1,0:T(8,128)(2,1)}, u32[]{:S(2)}) copy-start(bf16[1,128,1536]{2,1,0:T(8,128)(2,1)} %get-tuple-element.9) | copy-start | bytes 1179652
  34.0 1.1 %copy-start = (bf16[1,128,1536]{2,1,0:T(8,128)(2,1)S(1)}, bf16[1,128,1536]{2,1,0:T(8,128)(2,1)}, u32[]{:S(2)}) copy-start(bf16[1,128,1536]{2,1,0:T(8,128)(2,1)} %get-tuple-element.10) | copy-start | bytes 1179652
  35.2 0.8 %copy-start.2 = (f32[2,128]{1,0:T(2,128)S(1)}, f32[2,128]{1,0:T(2,128)}, u32[]{:S(2)}) copy-start(f32[2,128]{1,0:T(2,128)} %get-tuple-element.11) | copy-start | bytes 3076

commit v2 on v1

--- a/solution.py
+++ b/solution.py
@@ -21,10 +21,10 @@
 
 def kernel(
     rows, width, samples, n_seq, n_dp,
-    q_ref, k_ref, v_ref, g_ref, qgain_ref, kgain_ref, len_ref,
+    q_ref, k_ref, v_ref, g_ref, qgain_in, kgain_in, len_in,
     dq_ref, dk_ref, dv_ref, gain_ref,
-    win, bias, owned, own_out, ret_send, ret_recv, gain_acc, seq_gain, dp_gain,
-    load_sem, send_sem, recv_sem, back_send_sem, back_recv_sem, store_sem,
+    qgain_ref, kgain_ref, len_ref, win, bias, owned, ret_send, ret_recv, gain_acc, seq_gain, dp_gain,
+    load_sem, send_sem, recv_sem, back_send_sem, back_recv_sem,
     seq_send_sem, seq_recv_sem, dp_send_sem, dp_recv_sem,
 ):
     half = rows // 2
@@ -49,6 +49,14 @@
         pltpu.make_async_copy(ref.at[0], win.at[a, pl.ds(half, rows)], load_sem.at[a])
         for a, ref in enumerate(inputs)
     ]
+    small = [
+        pltpu.make_async_copy(src, dst, load_sem.at[4 + i])
+        for i, (src, dst) in enumerate(
+            ((len_in, len_ref), (qgain_in, qgain_ref), (kgain_in, kgain_ref))
+        )
+    ]
+    for load in small:
+        load.start()
     for load in loads:
         load.start()
     pl.semaphore_wait(barrier, n_seq + n_dp - 2)
@@ -110,6 +118,8 @@
         win[:, half + rows:, :] = jnp.zeros((4, half, width), jnp.bfloat16)
         ret_recv[1] = jnp.zeros((3, half, width), jnp.bfloat16)
 
+    for load in small:
+        load.wait()
     first = me * rows
     base = first - half
     far = rows * n_seq + window
@@ -170,7 +180,7 @@
         dk = norm_back(dk, k_unit, k_inv, k_gain)
         for a, out in enumerate((dq, dk, dv)):
             ret_send[0, a, :, cols] = out[:half]
-            own_out[a, :, cols] = out[half:half + rows]
+            outputs[a][0, :, cols] = out[half:half + rows]
             ret_send[1, a, :, cols] = out[half + rows:]
 
     @pl.loop(0, steps)
@@ -196,23 +206,29 @@
         def _():
             back_left(step).start()
 
-    seq_gain[me] = gain_acc[...]
-    for d in range(1, n_seq):
-        peer = lax.rem(me + d, n_seq)
-        pltpu.make_async_remote_copy(
-            seq_gain.at[me], seq_gain.at[me], seq_send_sem.at[d], seq_recv_sem.at[me],
-            device_id={"seq": peer},
-        ).start()
-
-    def stores(step):
-        return [
-            pltpu.make_async_copy(
-                own_out.at[a, :, columns(step)],
-                outputs[a].at[0, :, columns(step)],
-                store_sem.at[step, a],
+    def exchange(slots, axis, mine, count, send_sems, recv_sems):
+        def copy(d, slot):
+            return pltpu.make_async_remote_copy(
+                slots.at[mine], slots.at[slot], send_sems.at[d], recv_sems.at[slot],
+                device_id={axis: lax.rem(mine + d, count)},
             )
-            for a in range(3)
-        ]
+
+        def start():
+            for d in range(1, count):
+                copy(d, mine).start()
+
+        def wait():
+            for d in range(1, count):
+                copy(d, lax.rem(mine + d, count)).wait()
+            total = slots[0]
+            for i in range(1, count):
+                total = total + slots[i]
+            return total
+
+        return start, wait
+
+    dp_start, dp_wait = exchange(dp_gain, "dp", my_dp, n_dp, dp_send_sem, dp_recv_sem)
+    seq_start, seq_wait = exchange(seq_gain, "seq", me, n_seq, seq_send_sem, seq_recv_sem)
 
     def merge(step):
         @pl.when(has_left)
@@ -224,44 +240,25 @@
             back_left(step).wait_recv()
 
         cols = columns(step)
-        own_out[:, 0:half, cols] += ret_recv[0, :, :, cols]
-        own_out[:, half:rows, cols] += ret_recv[1, :, :, cols]
-        for store in stores(step):
-            store.start()
-
-    @pl.loop(0, steps - 1)
+        for a, out in enumerate(outputs):
+            out[0, 0:half, cols] += ret_recv[0, a, :, cols]
+            out[0, half:rows, cols] += ret_recv[1, a, :, cols]
+
+    dp_gain[my_dp] = gain_acc[...]
+    dp_start()
+
+    @pl.loop(0, steps - 2)
     def _(step):
         merge(step)
 
-    summed = jnp.zeros_like(gain_acc)
-    for d in range(1, n_seq):
-        peer = lax.rem(me + d, n_seq)
-        pltpu.make_async_remote_copy(
-            seq_gain.at[me], seq_gain.at[peer], seq_send_sem.at[d], seq_recv_sem.at[peer],
-            device_id={"seq": peer},
-        ).wait()
-    for i in range(n_seq):
-        summed = summed + seq_gain[i]
-    dp_gain[my_dp] = summed
-    for d in range(1, n_dp):
-        peer = lax.rem(my_dp + d, n_dp)
-        pltpu.make_async_remote_copy(
-            dp_gain.at[my_dp], dp_gain.at[my_dp], dp_send_sem.at[d], dp_recv_sem.at[my_dp],
-            device_id={"dp": peer},
-        ).start()
-
-    merge(steps - 1)
-
-    for d in range(1, n_dp):
-        peer = lax.rem(my_dp + d, n_dp)
-        pltpu.make_async_remote_copy(
-            dp_gain.at[my_dp], dp_gain.at[peer], dp_send_sem.at[d], dp_recv_sem.at[peer],
-            device_id={"dp": peer},
-        ).wait()
-    summed = jnp.zeros_like(gain_acc)
-    for i in range(n_dp):
-        summed = summed + dp_gain[i]
-    gain_ref[...] = summed[0:2]
+    seq_gain[me] = dp_wait()
+    seq_start()
+
+    @pl.loop(steps - 2, steps)
+    def _(step):
+        merge(step)
+
+    gain_ref[...] = seq_wait()
 
     @pl.loop(0, steps)
     def _(step):
@@ -277,8 +274,18 @@
                 to_left(a, step).wait_send()
             back_left(step).wait_send()
 
-        for store in stores(step):
-            store.wait()
+
+def write_back(dq_in, dk_in, dv_in, gain_in, dq_ref, dk_ref, dv_ref, gain_ref, sem):
+    copies = [
+        pltpu.make_async_copy(held, out, sem.at[i])
+        for i, (held, out) in enumerate(
+            ((dq_in, dq_ref), (dk_in, dk_ref), (dv_in, dv_ref), (gain_in, gain_ref))
+        )
+    ]
+    for copy in copies:
+        copy.start()
+    for copy in copies:
+        copy.wait()
 
 
 def body(query_rows, key_rows, value_rows, out_grad, query_gain, key_gain, lengths):
@@ -289,39 +296,51 @@
     steps = width // (HEADS_STEP * DH)
     big = jax.ShapeDtypeStruct((1, rows, width), jnp.bfloat16)
     anywhere = pl.BlockSpec(memory_space=pl.ANY)
+    hbm = pl.BlockSpec(memory_space=pltpu.HBM)
     vmem = pl.BlockSpec(memory_space=pltpu.VMEM)
     dma = pltpu.SemaphoreType.DMA
-    return pl.pallas_call(
+    limit = 67043328 - 3 * big.size * 2 - 131072
+    shapes = (big, big, big, jax.ShapeDtypeStruct((2, DH), jnp.float32))
+    results = pl.pallas_call(
         functools.partial(kernel, rows, width, samples, n_seq, n_dp),
-        out_shape=(big, big, big, jax.ShapeDtypeStruct((2, DH), jnp.float32)),
-        in_specs=[anywhere] * 4 + [vmem] * 2 + [pl.BlockSpec(memory_space=pltpu.SMEM)],
-        out_specs=(anywhere, anywhere, anywhere, vmem),
+        out_shape=tuple(pltpu.VMEM(x.shape, x.dtype) for x in shapes),
+        in_specs=[hbm] * 4 + [hbm] * 3,
+        out_specs=(vmem, vmem, vmem, vmem),
         scratch_shapes=[
+            pltpu.VMEM((1, DH), jnp.float32),
+            pltpu.VMEM((1, DH), jnp.float32),
+            pltpu.SMEM((1, samples), jnp.int32),
             pltpu.VMEM((4, window, width), jnp.bfloat16),
             pltpu.VMEM((window, window), jnp.float32),
             pltpu.VMEM((window, 1), jnp.float32),
-            pltpu.VMEM((3, rows, width), jnp.bfloat16),
             pltpu.VMEM((2, 3, half, width), jnp.bfloat16),
             pltpu.VMEM((2, 3, half, width), jnp.bfloat16),
-            pltpu.VMEM((8, DH), jnp.float32),
-            pltpu.VMEM((n_seq, 8, DH), jnp.float32),
-            pltpu.VMEM((n_dp, 8, DH), jnp.float32),
-            dma((4,)),
+            pltpu.VMEM((2, DH), jnp.float32),
+            pltpu.VMEM((n_seq, 2, DH), jnp.float32),
+            pltpu.VMEM((n_dp, 2, DH), jnp.float32),
+            dma((7,)),
             dma((steps, 4, 2)),
             dma((steps, 4, 2)),
             dma((steps, 2)),
             dma((steps, 2)),
-            dma((steps, 3)),
             dma((n_seq,)),
             dma((n_seq,)),
             dma((n_dp,)),
             dma((n_dp,)),
         ],
-        compiler_params=pltpu.CompilerParams(collective_id=0, has_side_effects=True),
+        compiler_params=pltpu.CompilerParams(collective_id=0, has_side_effects=True, vmem_limit_bytes=limit),
     )(
         query_rows, key_rows, value_rows, out_grad,
         query_gain.reshape(1, DH), key_gain.reshape(1, DH), lengths,
     )
+    return pl.pallas_call(
+        write_back,
+        out_shape=shapes,
+        in_specs=[anywhere] * 4,
+        out_specs=(anywhere,) * 4,
+        scratch_shapes=[dma((4,))],
+        compiler_params=pltpu.CompilerParams(vmem_limit_bytes=8 << 20),
+    )(*results)
 
 
 def solution(mesh):

time: 36.7 us -> 30.6 us (0.83)
  local copies, waits for them, and re-layouts: 4.27 us -> 0 us
  Pallas kernels: 31.6 us -> 29.8 us
    unnamed x10 -> x0, local copies, waits for them, and re-layouts: 4.27 us -> none
    pallas_call x1, Pallas kernels: 31.6 us -> 28.8 us  [body(): pl.pallas_call(functools.partial(kernel, rows, width, samples, n_seq, n_d...]
    pallas_call x0 -> x1, Pallas kernels: none -> 1.04 us  [body(): pl.pallas_call(write_back, out_shape=shapes, in_specs=[anywhere] * 4, out...]
where the time goes in v2:
time: 30.6 us; the launch traced here: 30.5 us
  Pallas kernels  29.8 us (97%)
  between operations  0.64 us (2%)
    pallas_call x1, Pallas kernels, body(): pl.pallas_call(functools.partial(kernel, rows, width, samples, n_seq, n_d...  28.8 us
    pallas_call x1, Pallas kernels, body(): pl.pallas_call(write_back, out_shape=shapes, in_specs=[anywhere] * 4, out...  1.04 us

profile of v2, /device:TPU:0, one launch (start us, length us, event | category | flops | bytes accessed | tf_op | source)
XLA Modules:
  0.0 30.5 jit_solution(17047989211889462161)
XLA Ops:
  0.6 28.8 %shard_map.102 = (bf16[1,128,1536]{2,1,0:T(8,128)(2,1)S(1)}, bf16[1,128,1536]{2,1,0:T(8,128)(2,1)S(1)}, bf16[1,128,1536]{2,1,0:T(8,128)(2,1)S(1)}, f32[2,128]{1,0:T(2,128)S(1)}) custom-call(bf16[1,128,1536]{2,1,0:T(8,128)(2,1)} %q_ref.1, bf16[1,128,1536]{2,1,0:T(8,128)(2,1)} %k_ref.1, bf16[1,128,1536]{2,1,0:T(8,128)(2,1)} %v_ref.1, ...), custom_call_target="tpu_custom_call" | custom-call | tf_op jit(solution)/shard_map/pallas_call | solution.py:304
  29.4 1.0 %shard_map.103 = (bf16[1,128,1536]{2,1,0:T(8,128)(2,1)}, bf16[1,128,1536]{2,1,0:T(8,128)(2,1)}, bf16[1,128,1536]{2,1,0:T(8,128)(2,1)}, f32[2,128]{1,0:T(2,128)}) custom-call(bf16[1,128,1536]{2,1,0:T(8,128)(2,1)S(1)} %get-tuple-element.8.dq_in, bf16[1,128,1536]{2,1,0:T(8,128)(2,1)S(1)} %get-tuple-element.9.dk_in, ...), custom_call_target="tpu_custom_call" | custom-call | tf_op jit(solution)/shard_map/pallas_call | solution.py:336

commit v3 on v2

--- a/solution.py
+++ b/solution.py
@@ -10,7 +10,7 @@
 DH = 128
 EPSILON = 1e-06
 MASKED = -1e30
-HEADS_STEP = 2
+HEADS_STEP = 3
 
 
 def norm_back(grad, unit, inverse, gain):
@@ -171,13 +171,13 @@
         row_dot = jnp.sum(grad.astype(jnp.float32) * attended, axis=1, keepdims=True)
         grad_weights = dot(grad, v, rowrow)
         grad_scores = (weights * (grad_weights - row_dot)).astype(jnp.bfloat16)
-        dq = jnp.dot(grad_scores, k_norm, preferred_element_type=jnp.float32) * factor
-        dk = dot(grad_scores, q_norm, colcol) * factor
+        dq = jnp.dot(grad_scores, k_norm, preferred_element_type=jnp.float32)
+        dk = dot(grad_scores, q_norm, colcol)
         dv = dot(half_weights, grad, colcol).astype(jnp.bfloat16)
         gain_acc[0:1] += jnp.sum(dq * q_unit, axis=0, keepdims=True)
         gain_acc[1:2] += jnp.sum(dk * k_unit, axis=0, keepdims=True)
-        dq = norm_back(dq, q_unit, q_inv, q_gain)
-        dk = norm_back(dk, k_unit, k_inv, k_gain)
+        dq = norm_back(dq, q_unit, q_inv, q_gain * factor)
+        dk = norm_back(dk, k_unit, k_inv, k_gain * factor)
         for a, out in enumerate((dq, dk, dv)):
             ret_send[0, a, :, cols] = out[:half]
             outputs[a][0, :, cols] = out[half:half + rows]
@@ -244,7 +244,7 @@
             out[0, 0:half, cols] += ret_recv[0, a, :, cols]
             out[0, half:rows, cols] += ret_recv[1, a, :, cols]
 
-    dp_gain[my_dp] = gain_acc[...]
+    dp_gain[my_dp] = gain_acc[...] * factor
     dp_start()
 
     @pl.loop(0, steps - 2)

time: 30.6 us -> 30.3 us (level)
    pallas_call x1, Pallas kernels: 28.8 us -> 28.4 us  [body(): pl.pallas_call(functools.partial(kernel, rows, width, samples, n_seq, n_d...]
where the time goes in v3:
time: 30.3 us; the launch traced here: 30.1 us
  Pallas kernels  29.5 us (97%)
  between operations  0.64 us (2%)
    pallas_call x1, Pallas kernels, body(): pl.pallas_call(functools.partial(kernel, rows, width, samples, n_seq, n_d...  28.4 us
    pallas_call x1, Pallas kernels, body(): pl.pallas_call(write_back, out_shape=shapes, in_specs=[anywhere] * 4, out...  1.04 us

profile of v3, /device:TPU:0, one launch (start us, length us, event | category | flops | bytes accessed | tf_op | source)
XLA Modules:
  0.0 30.1 jit_solution(4095404396914383224)
XLA Ops:
  0.6 28.4 %shard_map.102 = (bf16[1,128,1536]{2,1,0:T(8,128)(2,1)S(1)}, bf16[1,128,1536]{2,1,0:T(8,128)(2,1)S(1)}, bf16[1,128,1536]{2,1,0:T(8,128)(2,1)S(1)}, f32[2,128]{1,0:T(2,128)S(1)}) custom-call(bf16[1,128,1536]{2,1,0:T(8,128)(2,1)} %q_ref.1, bf16[1,128,1536]{2,1,0:T(8,128)(2,1)} %k_ref.1, bf16[1,128,1536]{2,1,0:T(8,128)(2,1)} %v_ref.1, ...), custom_call_target="tpu_custom_call" | custom-call | tf_op jit(solution)/shard_map/pallas_call | solution.py:304
  29.1 1.0 %shard_map.103 = (bf16[1,128,1536]{2,1,0:T(8,128)(2,1)}, bf16[1,128,1536]{2,1,0:T(8,128)(2,1)}, bf16[1,128,1536]{2,1,0:T(8,128)(2,1)}, f32[2,128]{1,0:T(2,128)}) custom-call(bf16[1,128,1536]{2,1,0:T(8,128)(2,1)S(1)} %get-tuple-element.8.dq_in, bf16[1,128,1536]{2,1,0:T(8,128)(2,1)S(1)} %get-tuple-element.9.dk_in, ...), custom_call_target="tpu_custom_call" | custom-call | tf_op jit(solution)/shard_map/pallas_call | solution.py:336
